TPU v7x, 32 devices: a whole 2x2x4 slice. The times are simulated.
32 devices in a mesh: expert: 2 (over y), hidden: 4 (over z), dp: 4 (over x, core).
Axes of the slice: x: 2, y: 2, z: 4, core: 2. Of those that a mesh axis runs over, the one named last changes fastest.
Arguments:
- tokens: bfloat16 [2, 4, 512, 2048], P('expert', 'dp', None, 'hidden'), may hold values from -6 to 6
- grad_out: bfloat16 [2, 4, 512, 2048], P('expert', 'dp', None, 'hidden'), may hold values from -0.25 to 0.25
- gate_weight: bfloat16 [4, 2048, 512], P('expert', 'dp', 'hidden'), may hold values from -0.125 to 0.125
- up_weight: bfloat16 [4, 2048, 512], P('expert', 'dp', 'hidden'), may hold values from -0.125 to 0.125
- down_weight: bfloat16 [4, 512, 2048], P('expert', 'hidden', 'dp'), may hold values from -0.25 to 0.25
- matching: int32 [2], replicated, may hold values from 0 to 1, each once
- block_counts: int32 [2, 4, 2], P('expert', 'dp'), may hold values from 0 to 4, as said below
Outputs:
- grad_gate: bfloat16 [4, 2048, 512], P('expert', 'dp', 'hidden')
- grad_up: bfloat16 [4, 2048, 512], P('expert', 'dp', 'hidden')
- grad_down: bfloat16 [4, 512, 2048], P('expert', 'hidden', 'dp')
Inputs may be any that keep to these rules, and one draw needn't show every extreme that they name: `matching`: each expert index appears once. `block_counts`: the 2 counts of one expert index and data index sum to at most 4; on some device one count equals 4.
All inputs are finite; a program needn't handle non-finite values.
Results may differ from a plain program's by a relative error of at most 0.008.
Values may be sent and summed in bfloat16 or wider, within the bound.
A program may use at most 64 MiB of HBM per device.

v0:
```python
import jax
import jax.numpy as jnp
from jax import lax
from jax.sharding import PartitionSpec as P

BLOCK = 128


def contract_rows(left, right):
    return lax.dot_general(
        left, right, (((0,), (0,)), ((), ())), preferred_element_type=jnp.float32
    )


def block_owners(counts, blocks):
    bounds = jnp.cumsum(counts)
    index = jnp.arange(blocks, dtype=jnp.int32)
    owner = jnp.sum((index[:, None] >= bounds[None, :]).astype(jnp.int32), axis=1)
    owner = jnp.minimum(owner, counts.shape[0] - 1)
    alive = (index < bounds[-1]).astype(jnp.float32)
    return (owner, alive)


def add_into(total, term, expert):
    current = lax.dynamic_index_in_dim(total, expert, 0, keepdims=True)
    return lax.dynamic_update_index_in_dim(total, current + term[None], expert, 0)


def expert_terms(row_blocks, grad_blocks, weight_gate, weight_up, weight_down, owner, alive):
    zeros_gate = jnp.zeros(weight_gate.shape, jnp.float32)
    zeros_down = jnp.zeros(weight_down.shape, jnp.float32)

    def step(carry, inputs):
        total_gate, total_up, total_down = carry
        row_block, grad_block, expert, live = inputs
        gate_matrix = lax.dynamic_index_in_dim(weight_gate, expert, 0, keepdims=False)
        up_matrix = lax.dynamic_index_in_dim(weight_up, expert, 0, keepdims=False)
        down_matrix = lax.dynamic_index_in_dim(weight_down, expert, 0, keepdims=False)
        gate_value = jnp.dot(row_block, gate_matrix, preferred_element_type=jnp.float32)
        up_value = jnp.dot(row_block, up_matrix, preferred_element_type=jnp.float32)
        sigmoid_gate = jax.nn.sigmoid(gate_value)
        activated = gate_value * sigmoid_gate
        hidden = (activated * up_value * live).astype(jnp.bfloat16)
        grad_hidden = lax.dot_general(
            grad_block, down_matrix, (((1,), (1,)), ((), ())), preferred_element_type=jnp.float32
        )
        grad_gate = (
            grad_hidden * up_value * sigmoid_gate * (1.0 + gate_value * (1.0 - sigmoid_gate)) * live
        ).astype(jnp.bfloat16)
        grad_up = (grad_hidden * activated * live).astype(jnp.bfloat16)
        total_gate = add_into(total_gate, contract_rows(row_block, grad_gate), expert)
        total_up = add_into(total_up, contract_rows(row_block, grad_up), expert)
        total_down = add_into(total_down, contract_rows(hidden, grad_block), expert)
        return ((total_gate, total_up, total_down), None)

    totals, unused = lax.scan(
        step, (zeros_gate, zeros_gate, zeros_down), (row_blocks, grad_blocks, owner, alive)
    )
    return totals


def relocate(arrays, matching):
    groups = lax.axis_size("expert")
    joined = jnp.concatenate([array_piece.reshape(groups, -1) for array_piece in arrays], axis=1)
    spread = lax.all_to_all(joined, "expert", split_axis=0, concat_axis=0, tiled=True)
    ordered = jnp.take(spread, matching, axis=0)
    settled = lax.all_to_all(ordered, "expert", split_axis=0, concat_axis=0, tiled=True)
    pieces = []
    offset = 0
    for array_piece in arrays:
        length = array_piece.size // groups
        pieces.append(settled[:, offset : offset + length].reshape(array_piece.shape))
        offset = offset + length
    return pieces


def on_device(tokens, grad_out, gate_weight, up_weight, down_weight, matching, block_counts):
    moved = relocate((gate_weight, up_weight, down_weight), matching)
    weight_gate, weight_up, weight_down = (
        lax.all_gather(moved[0], "dp", axis=1, tiled=True),
        lax.all_gather(moved[1], "dp", axis=1, tiled=True),
        lax.all_gather(moved[2], "dp", axis=2, tiled=True),
    )
    rows_full, grads_full = (
        lax.all_gather(tokens[0, 0], "hidden", axis=1, tiled=True),
        lax.all_gather(grad_out[0, 0], "hidden", axis=1, tiled=True),
    )
    blocks = rows_full.shape[0] // BLOCK
    width = rows_full.shape[1]
    owner, alive = block_owners(block_counts[0, 0], blocks)
    totals = expert_terms(
        rows_full.reshape(blocks, BLOCK, width),
        grads_full.reshape(blocks, BLOCK, width),
        weight_gate,
        weight_up,
        weight_down,
        owner,
        alive,
    )
    summed = (
        lax.psum_scatter(
            totals[0].astype(jnp.bfloat16), "dp", scatter_dimension=1, tiled=True
        ).astype(jnp.float32),
        lax.psum_scatter(
            totals[1].astype(jnp.bfloat16), "dp", scatter_dimension=1, tiled=True
        ).astype(jnp.float32),
        lax.psum_scatter(
            totals[2].astype(jnp.bfloat16), "dp", scatter_dimension=2, tiled=True
        ).astype(jnp.float32),
    )
    return (
        summed[0].astype(jnp.bfloat16),
        summed[1].astype(jnp.bfloat16),
        summed[2].astype(jnp.bfloat16),
    )


def solution(mesh):
    in_specs = (
        P("expert", "dp", None, "hidden"),
        P("expert", "dp", None, "hidden"),
        P("expert", "dp", "hidden"),
        P("expert", "dp", "hidden"),
        P("expert", "hidden", "dp"),
        P(),
        P("expert", "dp", None),
    )
    out_specs = (
        P("expert", "dp", "hidden"),
        P("expert", "dp", "hidden"),
        P("expert", "hidden", "dp"),
    )
    return jax.shard_map(
        on_device, mesh=mesh, in_specs=in_specs, out_specs=out_specs, check_vma=False
    )
```

profile of v0, /device:TPU:0, one launch (start us, length us, event | category | flops | bytes accessed | tf_op | source)
XLA Modules:
  0.0 368.9 jit_solution(15848804387790991597)
XLA Ops:
  8.4 1.6 copy_bitcast_fusion.5
  10.0 9.9 %maximum_bitcast_fusion = bf16[2,1,196608]{2,0,1:T(2,128)(2,1)S(1)} fusion(bf16[2,65536]{1,0:T(2,128)(2,1)S(1)} %bitcast.118, bf16[2,65536]{1,0:T(2,128)(2,1)S(1)} %get-tuple-element.92, bf16[2,65536]{1,0:T(2,128)(2,1)S(1)} %get-tuple-element.93), kind=kLoop, calls=%fused_computation.51 | loop fusion | flops 2359296 | bytes 1572864 | tf_op jit(solution)/shard_map/all_to_all | solution.py:65
  20.4 2.6 reduce
  23.0 1.5 reshape.103
  24.5 4.3 %all-to-all-start = ((bf16[2,2,98304]{2,1,0:T(2,128)(2,1)}), bf16[2,2,98304]{2,1,0:T(2,128)(2,1)S(1)}, u32[]{:S(2)}, u32[]{:S(2)}) async-start(bf16[2,2,98304]{2,1,0:T(2,128)(2,1)} %reshape.103), calls=%async_computation | async-start | bytes 1572864 | tf_op jit(solution)/shard_map/all_to_all | solution.py:65
  28.8 11.5 %all-to-all-done = bf16[2,2,98304]{2,1,0:T(2,128)(2,1)S(1)} async-done(((bf16[2,2,98304]{2,1,0:T(2,128)(2,1)}), bf16[2,2,98304]{2,1,0:T(2,128)(2,1)S(1)}, u32[]{:S(2)}, u32[]{:S(2)}) %all-to-all-start) | async-done | bytes 786464 | tf_op jit(solution)/shard_map/all_to_all | solution.py:65
  41.0 2.5 copy.31
  46.2 7.0 %broadcast_select_fusion = bf16[2,1,196608]{2,0,1:T(2,128)(2,1)S(1)} fusion(pred[2]{0:T(512)(128)(4,1)S(1)} %compare_and_fusion, bf16[2,98304]{1,0:T(2,128)(2,1)S(1)} %gather_fusion.1, bf16[2,98304]{1,0:T(2,128)(2,1)S(1)} %gather_fusion), kind=kLoop, calls=%fused_computation.50 | loop fusion | flops 1966080 | bytes 1572866 | tf_op jit(solution)/shard_map/jit(_take)/select_n | solution.py:66
  53.2 2.6 reduce.1
  56.4 12.9 %all_to_all.21 = bf16[2,2,98304]{2,1,0:T(2,128)(2,1)S(1)} all-to-all(bf16[2,2,98304]{2,1,0:T(2,128)(2,1)S(1)} %reshape.105), channel_id=1, replica_groups=mesh['expert'=2,'hidden'=4,'dp'=4] {'expert'}, dimensions={0} | all-to-all | bytes 1572864 | tf_op jit(solution)/shard_map/all_to_all | solution.py:67
  70.0 2.5 copy.30
  78.3 12.6 %all-gather.12.cloned.1.call-done = bf16[2,2048,128]{2,1,0:T(8,128)(2,1)} async-done(((bf16[2,512,128]{2,1,0:T(8,128)(2,1)}), bf16[2,2048,128]{2,1,0:T(8,128)(2,1)}) %all-gather.12.cloned.1.call-update) | async-done | bytes 1048592 | tf_op jit(solution)/shard_map/all_gather | solution.py:80
  90.9 18.9 %all-gather.10.cloned.1.call-done = bf16[2,2048,128]{2,1,0:T(8,128)(2,1)} async-done(((bf16[2,512,128]{2,1,0:T(8,128)(2,1)}), bf16[2,2048,128]{2,1,0:T(8,128)(2,1)}) %all-gather.10.cloned.1.call-update) | async-done | bytes 1048592 | tf_op jit(solution)/shard_map/all_gather | solution.py:81
  109.8 18.9 %all-gather.8.cloned.1.call-done = bf16[2,128,2048]{2,1,0:T(8,128)(2,1)} async-done(((bf16[2,128,512]{2,1,0:T(8,128)(2,1)}), bf16[2,128,2048]{2,1,0:T(8,128)(2,1)}) %all-gather.8.cloned.1.call-update) | async-done | bytes 1048592 | tf_op jit(solution)/shard_map/all_gather | solution.py:82
  128.7 47.1 %all-gather.14.cloned.1.call-done = bf16[1,1,512,2048]{3,2,1,0:T(8,128)(2,1)} async-done(((bf16[1,1,512,512]{3,2,1,0:T(8,128)(2,1)}), bf16[1,1,512,2048]{3,2,1,0:T(8,128)(2,1)}) %all-gather.14.cloned.1.call-update) | async-done | bytes 2097168 | tf_op jit(solution)/shard_map/all_gather | solution.py:85
  175.8 45.9 %all-gather.16.cloned.1.call-done = bf16[1,1,512,2048]{3,2,1,0:T(8,128)(2,1)} async-done(((bf16[1,1,512,512]{3,2,1,0:T(8,128)(2,1)}), bf16[1,1,512,2048]{3,2,1,0:T(8,128)(2,1)}) %all-gather.16.cloned.1.call-update) | async-done | bytes 2097168 | tf_op jit(solution)/shard_map/all_gather | solution.py:86
  221.7 1.5 broadcast_in_dim.29.clone
  223.2 1.6 broadcast_in_dim.30
  226.2 53.4 %while.14 = (s32[]{:T(128)}, f32[2,2048,128]{2,1,0:T(8,128)}, f32[2,2048,128]{2,1,0:T(8,128)}, f32[2,128,2048]{2,1,0:T(8,128)}, s32[4]{0:T(128)S(1)}, /*index=5*...) while((s32[]{:T(128)}, f32[2,2048,128]{2,1,0:T(8,128)}, ...), condition=%wide.region_3.4_spmd, body=%wide.region_2.3_spmd.sunk | while | flops 403849216 | bytes 61997988 | solution.py:56
  231.0 1.7 fusion.70
  236.1 2.1 fusion.74
  244.3 1.6 fusion.70
  249.4 2.1 fusion.74
  257.7 1.7 fusion.70
  262.8 2.1 fusion.74
  271.0 1.7 fusion.70
  276.1 2.1 fusion.74
  279.6 2.7 convert_element_type.34
  282.4 2.9 convert_element_type.32
  286.5 19.6 %reduce-scatter.8.cloned.1.call-done = bf16[2,128,512]{2,1,0:T(8,128)(2,1)} async-done(((bf16[2,128,2048]{2,1,0:T(8,128)(2,1)}), bf16[2,128,512]{2,1,0:T(8,128)(2,1)}) %reduce-scatter.8.cloned.1.call-update) | async-done | bytes 262160 | tf_op jit(solution)/shard_map/reduce_scatter | solution.py:107
  306.1 27.9 %reduce-scatter.4.cloned.1.call-done = bf16[2,512,128]{2,1,0:T(8,128)(2,1)} async-done(((bf16[2,2048,128]{2,1,0:T(8,128)(2,1)}), bf16[2,512,128]{2,1,0:T(8,128)(2,1)}) %reduce-scatter.4.cloned.1.call-update) | async-done | bytes 262160 | tf_op jit(solution)/shard_map/reduce_scatter | solution.py:101
  334.1 27.9 %reduce-scatter.6.cloned.1.call-done = bf16[2,512,128]{2,1,0:T(8,128)(2,1)} async-done(((bf16[2,2048,128]{2,1,0:T(8,128)(2,1)}), bf16[2,512,128]{2,1,0:T(8,128)(2,1)}) %reduce-scatter.6.cloned.1.call-update) | async-done | bytes 262160 | tf_op jit(solution)/shard_map/reduce_scatter | solution.py:104
  (120 shorter events, 45.0 us)
Async XLA Ops:
  20.4 8.4 %copy-start.9 = (s32[2]{0:T(128)S(1)}, s32[2]{0:T(128)}, u32[]{:S(2)}) copy-start(s32[2]{0:T(128)} %param.14) | copy-start | bytes 28
  24.5 15.8 %all-to-all-start = ((bf16[2,2,98304]{2,1,0:T(2,128)(2,1)}), bf16[2,2,98304]{2,1,0:T(2,128)(2,1)S(1)}, u32[]{:S(2)}, u32[]{:S(2)}) async-start(bf16[2,2,98304]{2,1,0:T(2,128)(2,1)} %reshape.103), calls=%async_computation | async-start | bytes 1572864 | tf_op jit(solution)/shard_map/all_to_all | solution.py:65
  28.8 62.2 %all-gather.12.cloned.1.call-start = ((), (), s32[]{:S(2)}) async-start(), calls=%async_computation.7 | async-start | bytes 1310720 | tf_op jit(solution)/shard_map/all_gather | solution.py:80
  73.1 3.8 %copy-start.10 = (s32[1,1,2]{2,1,0:T(1,128)S(1)}, s32[1,1,2]{2,1,0:T(1,128)}, u32[]{:S(2)}) copy-start(s32[1,1,2]{2,1,0:T(1,128)} %param.15) | copy-start | bytes 28
  73.8 36.0 %all-gather.10.cloned.1.call-start = ((), (), s32[]{:S(2)}) async-start(), calls=%async_computation.6 | async-start | bytes 1310720 | tf_op jit(solution)/shard_map/all_gather | solution.py:81
  74.6 54.0 %all-gather.8.cloned.1.call-start = ((), (), s32[]{:S(2)}) async-start(), calls=%async_computation.5 | async-start | bytes 1310720 | tf_op jit(solution)/shard_map/all_gather | solution.py:82
  75.4 100.3 %all-gather.14.cloned.1.call-start = ((), (), s32[]{:S(2)}) async-start(), calls=%async_computation.11 | async-start | bytes 2621440 | tf_op jit(solution)/shard_map/all_gather | solution.py:85
  76.0 145.7 %all-gather.16.cloned.1.call-start = ((), (), s32[]{:S(2)}) async-start(), calls=%async_computation.12 | async-start | bytes 2621440 | tf_op jit(solution)/shard_map/all_gather | solution.py:86
  76.6 229.5 %reduce-scatter.8.cloned.1.call-start = ((), (), s32[]{:S(2)}) async-start(), calls=%async_computation.10 | async-start | bytes 1310720 | tf_op jit(solution)/shard_map/reduce_scatter | solution.py:107
  223.2 3.1 copy-start
  223.2 3.1 copy-start.8
  228.8 3.9 %copy-start.1 = (f32[2,2048,128]{2,1,0:T(8,128)S(1)}, f32[2,2048,128]{2,1,0:T(8,128)}, u32[]{:S(2)}) copy-start(f32[2,2048,128]{2,1,0:T(8,128)} %get-tuple-element.177) | copy-start | bytes 6291460 | tf_op jit(solution)/shard_map/while
  231.0 2.7 copy-start.6
  233.7 4.5 %copy-start.2 = (f32[2,2048,128]{2,1,0:T(8,128)}, f32[2,2048,128]{2,1,0:T(8,128)S(1)}, u32[]{:S(2)}) copy-start(f32[2,2048,128]{2,1,0:T(8,128)S(1)} %fusion.73) | copy-start | bytes 6291460 | tf_op jit(solution)/shard_map/while
  233.7 2.4 copy-start.4
  242.1 3.9 %copy-start.1 = (f32[2,2048,128]{2,1,0:T(8,128)S(1)}, f32[2,2048,128]{2,1,0:T(8,128)}, u32[]{:S(2)}) copy-start(f32[2,2048,128]{2,1,0:T(8,128)} %get-tuple-element.177) | copy-start | bytes 6291460 | tf_op jit(solution)/shard_map/while
  244.3 2.7 copy-start.6
  247.1 4.5 %copy-start.2 = (f32[2,2048,128]{2,1,0:T(8,128)}, f32[2,2048,128]{2,1,0:T(8,128)S(1)}, u32[]{:S(2)}) copy-start(f32[2,2048,128]{2,1,0:T(8,128)S(1)} %fusion.73) | copy-start | bytes 6291460 | tf_op jit(solution)/shard_map/while
  247.1 2.4 copy-start.4
  249.4 2.1 copy-start.7
  255.4 3.9 %copy-start.1 = (f32[2,2048,128]{2,1,0:T(8,128)S(1)}, f32[2,2048,128]{2,1,0:T(8,128)}, u32[]{:S(2)}) copy-start(f32[2,2048,128]{2,1,0:T(8,128)} %get-tuple-element.177) | copy-start | bytes 6291460 | tf_op jit(solution)/shard_map/while
  257.7 2.7 copy-start.6
  260.4 4.5 %copy-start.2 = (f32[2,2048,128]{2,1,0:T(8,128)}, f32[2,2048,128]{2,1,0:T(8,128)S(1)}, u32[]{:S(2)}) copy-start(f32[2,2048,128]{2,1,0:T(8,128)S(1)} %fusion.73) | copy-start | bytes 6291460 | tf_op jit(solution)/shard_map/while
  260.4 2.4 copy-start.4
  268.8 3.9 %copy-start.1 = (f32[2,2048,128]{2,1,0:T(8,128)S(1)}, f32[2,2048,128]{2,1,0:T(8,128)}, u32[]{:S(2)}) copy-start(f32[2,2048,128]{2,1,0:T(8,128)} %get-tuple-element.177) | copy-start | bytes 6291460 | tf_op jit(solution)/shard_map/while
  271.0 2.7 copy-start.6
  273.7 4.5 %copy-start.2 = (f32[2,2048,128]{2,1,0:T(8,128)}, f32[2,2048,128]{2,1,0:T(8,128)S(1)}, u32[]{:S(2)}) copy-start(f32[2,2048,128]{2,1,0:T(8,128)S(1)} %fusion.73) | copy-start | bytes 6291460 | tf_op jit(solution)/shard_map/while
  273.8 2.4 copy-start.4
  276.1 2.1 copy-start.7
  282.4 51.7 %reduce-scatter.4.cloned.1.call-start = ((), (), s32[]{:S(2)}) async-start(), calls=%async_computation.8 | async-start | bytes 1310720 | tf_op jit(solution)/shard_map/reduce_scatter | solution.py:101
  282.4 2.9 copy-start.3
  285.3 76.7 %reduce-scatter.6.cloned.1.call-start = ((), (), s32[]{:S(2)}) async-start(), calls=%async_computation.9 | async-start | bytes 1310720 | tf_op jit(solution)/shard_map/reduce_scatter | solution.py:104
  (6 other events, 9.7 us)
Sparse Core Ops, SparseCore 0:
  73.9 16.9 all-gather.11
  93.0 16.6 all-gather.9
  111.9 16.6 all-gather.7
  130.1 45.6 all-gather.13
  177.2 44.4 all-gather.15
  282.5 23.5 reduce-scatter.7
  309.2 24.8 reduce-scatter.3
  337.2 24.8 reduce-scatter.5
where the time goes:
time: 370 us; the launch traced here: 369 us
  waiting for transfers between devices  232 us (63%)
  local copies, waits for them, and re-layouts  36.9 us (10%)
  matrix products  30.5 us (8%)
  other arithmetic  29.7 us (8%)
  between operations  14.3 us (4%)
  blocking collectives  12.9 us (3%)
  loops' own time  8.17 us (2%)
  starting transfers between devices  4.77 us (1%)
    all_gather x1, waiting for transfers between devices, on_device(): lax.all_gather(tokens[0, 0], 'hidden', axis=1, tiled=True)  47.1 us
    all_gather x1, waiting for transfers between devices, on_device(): lax.all_gather(grad_out[0, 0], 'hidden', axis=1, tiled=True)  45.9 us
    reduce_scatter x1, waiting for transfers between devices, on_device(): lax.psum_scatter(totals[1].astype(jnp.bfloat16), 'dp', scatter_dimension=...  27.9 us
    reduce_scatter x1, waiting for transfers between devices, on_device(): lax.psum_scatter(totals[0].astype(jnp.bfloat16), 'dp', scatter_dimension=...  27.9 us
    reduce_scatter x1, waiting for transfers between devices, on_device(): lax.psum_scatter(totals[2].astype(jnp.bfloat16), 'dp', scatter_dimension=...  19.6 us
    all_gather x1, waiting for transfers between devices, on_device(): lax.all_gather(moved[2], 'dp', axis=2, tiled=True)  18.9 us
    all_gather x1, waiting for transfers between devices, on_device(): lax.all_gather(moved[1], 'dp', axis=1, tiled=True)  18.9 us
    dot_general x12, matrix products, contract_rows(): lax.dot_general(left, right, (((0,), (0,)), ((), ())), preferred_element_...  17.5 us
  transfers between devices with their start and end apart: 9, of which 9 were waited for; matrix products, arithmetic and copies ran while one was open for 2% of the time, Pallas kernels for 0%

commit v1 on v0

--- a/solution.py
+++ b/solution.py
@@ -1,9 +1,30 @@
+import functools
 import jax
 import jax.numpy as jnp
 from jax import lax
 from jax.sharding import PartitionSpec as P
 
 BLOCK = 128
+
+
+def pair_the_results(shard_in, comm_axis, along_dim):
+    current_value = jax.lax.psum(1, axis_name=comm_axis)
+    r_now = jax.lax.axis_index(comm_axis)
+    b_next, m_next, side_arr = (current_value, r_now, shard_in.shape[along_dim])
+    all_values, front = (shard_in, 1)
+    while front < b_next:
+        current_arr = jax.lax.ppermute(
+            all_values,
+            axis_name=comm_axis,
+            perm=tuple(((j0, (j0 - front) % b_next) for j0 in range(b_next))),
+        )
+        all_values = jnp.concatenate([all_values, current_arr], along_dim)
+        front = 2 * front
+    t1 = jnp.roll(all_values, m_next * side_arr, along_dim)
+    return t1
+
+
+show_sections = functools.partial(pair_the_results, comm_axis="hidden", along_dim=1)
 
 
 def contract_rows(left, right):
@@ -82,7 +103,7 @@
         lax.all_gather(moved[2], "dp", axis=2, tiled=True),
     )
     rows_full, grads_full = (
-        lax.all_gather(tokens[0, 0], "hidden", axis=1, tiled=True),
+        show_sections(tokens[0, 0]),
         lax.all_gather(grad_out[0, 0], "hidden", axis=1, tiled=True),
     )
     blocks = rows_full.shape[0] // BLOCK

time: 370 us -> 335 us (0.905)
  waiting for transfers between devices: 232 us -> 179 us
  matrix products: 30.5 us -> 51.4 us
  local copies, waits for them, and re-layouts: 36.9 us -> 27.4 us
  starting transfers between devices: 4.77 us -> 9.03 us
    ppermute x0 -> x2, waiting for transfers between devices: none -> 53 us  [pair_the_results(): jax.lax.ppermute(all_values, axis_name=comm_axis, perm=tuple(((j0, (j0 -...]
    all_gather x1 -> x0, waiting for transfers between devices: 47.1 us -> none  [on_device(): lax.all_gather(tokens[0, 0], 'hidden', axis=1, tiled=True)]
    dot_general x12, matrix products: 17.5 us -> 38.9 us  [contract_rows(): lax.dot_general(left, right, (((0,), (0,)), ((), ())), preferred_element_...]
    all_gather x1, waiting for transfers between devices: 18.9 us -> 0.02 us  [on_device(): lax.all_gather(moved[2], 'dp', axis=2, tiled=True)]
    all_gather x1, waiting for transfers between devices: 18.9 us -> 0.02 us  [on_device(): lax.all_gather(moved[1], 'dp', axis=1, tiled=True)]
    all_gather x1, waiting for transfers between devices: 12.6 us -> 0.02 us  [on_device(): lax.all_gather(moved[0], 'dp', axis=1, tiled=True)]
    while x48 -> x0, local copies, waits for them, and re-layouts: 10 us -> none
    reduce_scatter x1, waiting for transfers between devices: 27.9 us -> 18.3 us  [on_device(): lax.psum_scatter(totals[0].astype(jnp.bfloat16), 'dp', scatter_dimension=...]
  transfers between devices with their start and end apart: 9 -> 10, of which waited for: 9 -> 7; matrix products, arithmetic and copies ran while one was open for 2% -> 3% of each run, Pallas kernels for 0% -> 0%
where the time goes in v1:
time: 335 us; the launch traced here: 333 us
  waiting for transfers between devices  179 us (53%)
  matrix products  51.4 us (15%)
  other arithmetic  31.3 us (9%)
  local copies, waits for them, and re-layouts  27.4 us (8%)
  between operations  14.4 us (4%)
  blocking collectives  12.9 us (4%)
  starting transfers between devices  9.03 us (3%)
  loops' own time  7.87 us (2%)
    ppermute x2, waiting for transfers between devices, pair_the_results(): jax.lax.ppermute(all_values, axis_name=comm_axis, perm=tuple(((j0, (j0 -...  53 us
    all_gather x1, waiting for transfers between devices, on_device(): lax.all_gather(grad_out[0, 0], 'hidden', axis=1, tiled=True)  39.9 us
    dot_general x12, matrix products, contract_rows(): lax.dot_general(left, right, (((0,), (0,)), ((), ())), preferred_element_...  38.9 us
    reduce_scatter x1, waiting for transfers between devices, on_device(): lax.psum_scatter(totals[2].astype(jnp.bfloat16), 'dp', scatter_dimension=...  27.9 us
    reduce_scatter x1, waiting for transfers between devices, on_device(): lax.psum_scatter(totals[1].astype(jnp.bfloat16), 'dp', scatter_dimension=...  27.8 us
    reduce_scatter x1, waiting for transfers between devices, on_device(): lax.psum_scatter(totals[0].astype(jnp.bfloat16), 'dp', scatter_dimension=...  18.3 us
    all_to_all x1, blocking collectives, relocate(): lax.all_to_all(ordered, 'expert', split_axis=0, concat_axis=0, tiled=True)  12.9 us
    unnamed x24, local copies, waits for them, and re-layouts  12.7 us
  transfers between devices with their start and end apart: 10, of which 7 were waited for; matrix products, arithmetic and copies ran while one was open for 3% of the time, Pallas kernels for 0%

profile of v1, /device:TPU:0, one launch (start us, length us, event | category | flops | bytes accessed | tf_op | source)
XLA Modules:
  0.0 333.4 jit_solution(5477762657873851647)
XLA Ops:
  10.0 9.9 %maximum_bitcast_fusion = bf16[2,1,196608]{2,0,1:T(2,128)(2,1)S(1)} fusion(bf16[2,65536]{1,0:T(2,128)(2,1)S(1)} %bitcast.123, bf16[2,65536]{1,0:T(2,128)(2,1)S(1)} %get-tuple-element.92, bf16[2,65536]{1,0:T(2,128)(2,1)S(1)} %get-tuple-element.93), kind=kLoop, calls=%fused_computation.52 | loop fusion | flops 2359296 | bytes 1572864 | tf_op jit(solution)/shard_map/all_to_all | solution.py:86
  20.4 2.6 reduce
  24.5 4.3 %all-to-all-start = ((bf16[2,2,98304]{2,1,0:T(2,128)(2,1)}), bf16[2,2,98304]{2,1,0:T(2,128)(2,1)S(1)}, u32[]{:S(2)}, u32[]{:S(2)}) async-start(bf16[2,2,98304]{2,1,0:T(2,128)(2,1)} %reshape.101), calls=%async_computation | async-start | bytes 1572864 | tf_op jit(solution)/shard_map/all_to_all | solution.py:86
  28.8 11.5 %all-to-all-done = bf16[2,2,98304]{2,1,0:T(2,128)(2,1)S(1)} async-done(((bf16[2,2,98304]{2,1,0:T(2,128)(2,1)}), bf16[2,2,98304]{2,1,0:T(2,128)(2,1)S(1)}, u32[]{:S(2)}, u32[]{:S(2)}) %all-to-all-start) | async-done | bytes 786464 | tf_op jit(solution)/shard_map/all_to_all | solution.py:86
  41.0 2.5 copy.31
  46.2 7.0 %broadcast_select_fusion = bf16[2,1,196608]{2,0,1:T(2,128)(2,1)S(1)} fusion(pred[2]{0:T(512)(128)(4,1)S(1)} %compare_and_fusion, bf16[2,98304]{1,0:T(2,128)(2,1)S(1)} %gather_fusion.1, bf16[2,98304]{1,0:T(2,128)(2,1)S(1)} %gather_fusion), kind=kLoop, calls=%fused_computation.50 | loop fusion | flops 1966080 | bytes 1572866 | tf_op jit(solution)/shard_map/jit(_take)/select_n | solution.py:87
  53.2 2.6 reduce.1
  56.4 12.9 %all_to_all.21 = bf16[2,2,98304]{2,1,0:T(2,128)(2,1)S(1)} all-to-all(bf16[2,2,98304]{2,1,0:T(2,128)(2,1)S(1)} %reshape.103), channel_id=1, replica_groups=mesh['expert'=2,'hidden'=4,'dp'=4] {'expert'}, dimensions={0} | all-to-all | bytes 1572864 | tf_op jit(solution)/shard_map/all_to_all | solution.py:88
  70.0 2.5 copy.30
  76.1 3.8 %collective-permute-start = (bf16[512,512]{1,0:T(8,128)(2,1)S(1)}, bf16[512,512]{1,0:T(8,128)(2,1)S(1)}, u32[]{:S(2)}, u32[]{:S(2)}) collective-permute-start(bf16[512,512]{1,0:T(8,128)(2,1)S(1)} %bitcast.115), channel_id=1, source_target_pairs={{0,12},{4,0},{8,4},{12,8},{1,13},{5,1},{9,5},{13,9},{2,14},{6,2},{... | collective-permute-start | bytes 1572872 | tf_op jit(solution)/shard_map/ppermute | solution.py:16
  79.9 10.3 %collective-permute-done = bf16[512,512]{1,0:T(8,128)(2,1)S(1)} collective-permute-done((bf16[512,512]{1,0:T(8,128)(2,1)S(1)}, bf16[512,512]{1,0:T(8,128)(2,1)S(1)}, u32[]{:S(2)}, u32[]{:S(2)}) %collective-permute-start) | collective-permute-done | bytes 524320 | tf_op jit(solution)/shard_map/ppermute | solution.py:16
  92.6 42.7 %collective-permute-done.1 = bf16[512,1024]{1,0:T(8,128)(2,1)S(1)} collective-permute-done((bf16[512,1024]{1,0:T(8,128)(2,1)S(1)}, bf16[512,1024]{1,0:T(8,128)(2,1)S(1)}, u32[]{:S(2)}, u32[]{:S(2)}) %collective-permute-start.1) | collective-permute-done | bytes 1048608 | tf_op jit(solution)/shard_map/ppermute | solution.py:16
  135.8 39.9 %all-gather.12.cloned.1.call-done = bf16[1,1,512,2048]{3,2,1,0:T(8,128)(2,1)} async-done(((bf16[1,1,512,512]{3,2,1,0:T(8,128)(2,1)}), bf16[1,1,512,2048]{3,2,1,0:T(8,128)(2,1)}) %all-gather.12.cloned.1.call-update) | async-done | bytes 2097168 | tf_op jit(solution)/shard_map/all_gather | solution.py:107
  180.3 64.0 %while.14 = (s32[]{:T(128)}, f32[2,2048,128]{2,1,0:T(8,128)}, f32[2,2048,128]{2,1,0:T(8,128)}, f32[2,128,2048]{2,1,0:T(8,128)}, s32[4]{0:T(128)S(1)}, /*index=5*...) while((s32[]{:T(128)}, f32[2,2048,128]{2,1,0:T(8,128)}, ...), condition=%wide.region_3.4_spmd, body=%wide.region_2.3_spmd.sunk | while | flops 403849216 | bytes 11669723 | solution.py:77
  186.5 3.2 fusion.72
  189.7 3.2 fusion.73
  192.9 3.4 %fusion.74 = f32[2,128,2048]{2,1,0:T(8,128)} fusion(f32[2,128,2048]{2,1,0:T(8,128)} %get-tuple-element.178, s32[]{:T(128)S(6)} %select_n.55, bf16[4,128,2048]{2,1,0:T(8,128)(2,1)} %get-tuple-element.195, s32[]{:T(128)} %get-tuple-element.175, f32[128,128]{1,0:T(8,128)S(1)} %fusion.71, f32[]{:T(128)} %bitcast.112, f32[128,128]{1,0:T(8,128)S(1)} %fusion.69), kind=kOutput, calls=%fused_computation.10.clone.1 | convolution fusion | flops 67485696 | bytes 2753540 | tf_op jit(solution)/shard_map/while/body/eval_jaxpr/dot_general | solution.py:31
  202.5 3.2 fusion.72
  205.7 3.2 fusion.73
  208.9 3.4 %fusion.74 = f32[2,128,2048]{2,1,0:T(8,128)} fusion(f32[2,128,2048]{2,1,0:T(8,128)} %get-tuple-element.178, s32[]{:T(128)S(6)} %select_n.55, bf16[4,128,2048]{2,1,0:T(8,128)(2,1)} %get-tuple-element.195, s32[]{:T(128)} %get-tuple-element.175, f32[128,128]{1,0:T(8,128)S(1)} %fusion.71, f32[]{:T(128)} %bitcast.112, f32[128,128]{1,0:T(8,128)S(1)} %fusion.69), kind=kOutput, calls=%fused_computation.10.clone.1 | convolution fusion | flops 67485696 | bytes 2753540 | tf_op jit(solution)/shard_map/while/body/eval_jaxpr/dot_general | solution.py:31
  218.5 3.2 fusion.72
  221.7 3.2 fusion.73
  224.9 3.4 %fusion.74 = f32[2,128,2048]{2,1,0:T(8,128)} fusion(f32[2,128,2048]{2,1,0:T(8,128)} %get-tuple-element.178, s32[]{:T(128)S(6)} %select_n.55, bf16[4,128,2048]{2,1,0:T(8,128)(2,1)} %get-tuple-element.195, s32[]{:T(128)} %get-tuple-element.175, f32[128,128]{1,0:T(8,128)S(1)} %fusion.71, f32[]{:T(128)} %bitcast.112, f32[128,128]{1,0:T(8,128)S(1)} %fusion.69), kind=kOutput, calls=%fused_computation.10.clone.1 | convolution fusion | flops 67485696 | bytes 2753540 | tf_op jit(solution)/shard_map/while/body/eval_jaxpr/dot_general | solution.py:31
  234.5 3.2 fusion.72
  237.7 3.2 fusion.73
  240.9 3.4 %fusion.74 = f32[2,128,2048]{2,1,0:T(8,128)} fusion(f32[2,128,2048]{2,1,0:T(8,128)} %get-tuple-element.178, s32[]{:T(128)S(6)} %select_n.55, bf16[4,128,2048]{2,1,0:T(8,128)(2,1)} %get-tuple-element.195, s32[]{:T(128)} %get-tuple-element.175, f32[128,128]{1,0:T(8,128)S(1)} %fusion.71, f32[]{:T(128)} %bitcast.112, f32[128,128]{1,0:T(8,128)S(1)} %fusion.69), kind=kOutput, calls=%fused_computation.10.clone.1 | convolution fusion | flops 67485696 | bytes 2753540 | tf_op jit(solution)/shard_map/while/body/eval_jaxpr/dot_general | solution.py:31
  244.2 2.7 convert_element_type.32
  247.0 2.7 convert_element_type.33
  249.8 2.7 convert_element_type.34
  252.6 18.3 %reduce-scatter.4.cloned.1.call-done = bf16[2,512,128]{2,1,0:T(8,128)(2,1)} async-done(((bf16[2,2048,128]{2,1,0:T(8,128)(2,1)}), bf16[2,512,128]{2,1,0:T(8,128)(2,1)}) %reduce-scatter.4.cloned.1.call-update) | async-done | bytes 262160 | tf_op jit(solution)/shard_map/reduce_scatter | solution.py:122
  270.8 27.8 %reduce-scatter.6.cloned.1.call-done = bf16[2,512,128]{2,1,0:T(8,128)(2,1)} async-done(((bf16[2,2048,128]{2,1,0:T(8,128)(2,1)}), bf16[2,512,128]{2,1,0:T(8,128)(2,1)}) %reduce-scatter.6.cloned.1.call-update) | async-done | bytes 262160 | tf_op jit(solution)/shard_map/reduce_scatter | solution.py:125
  298.6 27.9 %reduce-scatter.8.cloned.1.call-done = bf16[2,128,512]{2,1,0:T(8,128)(2,1)} async-done(((bf16[2,128,2048]{2,1,0:T(8,128)(2,1)}), bf16[2,128,512]{2,1,0:T(8,128)(2,1)}) %reduce-scatter.8.cloned.1.call-update) | async-done | bytes 262160 | tf_op jit(solution)/shard_map/reduce_scatter | solution.py:128
  (79 shorter events, 37.5 us)
Async XLA Ops:
  20.4 8.4 %copy-start.2 = (s32[2]{0:T(128)S(1)}, s32[2]{0:T(128)}, u32[]{:S(2)}) copy-start(s32[2]{0:T(128)} %param.14) | copy-start | bytes 28
  24.5 15.8 %all-to-all-start = ((bf16[2,2,98304]{2,1,0:T(2,128)(2,1)}), bf16[2,2,98304]{2,1,0:T(2,128)(2,1)S(1)}, u32[]{:S(2)}, u32[]{:S(2)}) async-start(bf16[2,2,98304]{2,1,0:T(2,128)(2,1)} %reshape.101), calls=%async_computation | async-start | bytes 1572864 | tf_op jit(solution)/shard_map/all_to_all | solution.py:86
  28.8 107.0 %all-gather.10.cloned.1.call-start = ((), (), s32[]{:S(2)}) async-start(), calls=%async_computation.7 | async-start | bytes 1310720 | tf_op jit(solution)/shard_map/all_gather | solution.py:101
  72.5 3.6 %copy-start.1 = (bf16[1,1,512,512]{3,2,1,0:T(8,128)(2,1)S(1)}, bf16[1,1,512,512]{3,2,1,0:T(8,128)(2,1)}, u32[]{:S(2)}) copy-start(bf16[1,1,512,512]{3,2,1,0:T(8,128)(2,1)} %param.9) | copy-start | bytes 1572868
  73.8 62.0 %all-gather.6.cloned.1.call-start = ((), (), s32[]{:S(2)}) async-start(), calls=%async_computation.5 | async-start | bytes 1310720 | tf_op jit(solution)/shard_map/all_gather | solution.py:103
  73.9 17.2 %copy-start.3 = (s32[1,1,2]{2,1,0:T(1,128)S(1)}, s32[1,1,2]{2,1,0:T(1,128)}, u32[]{:S(2)}) copy-start(s32[1,1,2]{2,1,0:T(1,128)} %param.15) | copy-start | bytes 28
  74.6 61.2 %all-gather.8.cloned.1.call-start = ((), (), s32[]{:S(2)}) async-start(), calls=%async_computation.6 | async-start | bytes 1310720 | tf_op jit(solution)/shard_map/all_gather | solution.py:102
  75.5 100.3 %all-gather.12.cloned.1.call-start = ((), (), s32[]{:S(2)}) async-start(), calls=%async_computation.11 | async-start | bytes 2621440 | tf_op jit(solution)/shard_map/all_gather | solution.py:107
  76.0 194.8 %reduce-scatter.4.cloned.1.call-start = ((), (), s32[]{:S(2)}) async-start(), calls=%async_computation.8 | async-start | bytes 1310720 | tf_op jit(solution)/shard_map/reduce_scatter | solution.py:122
  76.1 14.1 %collective-permute-start = (bf16[512,512]{1,0:T(8,128)(2,1)S(1)}, bf16[512,512]{1,0:T(8,128)(2,1)S(1)}, u32[]{:S(2)}, u32[]{:S(2)}) collective-permute-start(bf16[512,512]{1,0:T(8,128)(2,1)S(1)} %bitcast.115), channel_id=1, source_target_pairs={{0,12},{4,0},{8,4},{12,8},{1,13},{5,1},{9,5},{13,9},{2,14},{6,2},{... | collective-permute-start | bytes 1572872 | tf_op jit(solution)/shard_map/ppermute | solution.py:16
  90.4 44.9 %collective-permute-start.1 = (bf16[512,1024]{1,0:T(8,128)(2,1)S(1)}, bf16[512,1024]{1,0:T(8,128)(2,1)S(1)}, u32[]{:S(2)}, u32[]{:S(2)}) collective-permute-start(bf16[512,1024]{1,0:T(8,128)(2,1)S(1)} %pad_maximum_fusion), channel_id=1, source_target_pairs={{0,8},{4,12},{8,0},{12,4},{1,9},{5,13},{9,1},{13,5},{2,10},{6,14},... | collective-permute-start | bytes 3145736 | tf_op jit(solution)/shard_map/ppermute | solution.py:16
  177.2 3.0 copy-start
  247.0 51.7 %reduce-scatter.6.cloned.1.call-start = ((), (), s32[]{:S(2)}) async-start(), calls=%async_computation.9 | async-start | bytes 1310720 | tf_op jit(solution)/shard_map/reduce_scatter | solution.py:125
  249.8 76.8 %reduce-scatter.8.cloned.1.call-start = ((), (), s32[]{:S(2)}) async-start(), calls=%async_computation.10 | async-start | bytes 1310720 | tf_op jit(solution)/shard_map/reduce_scatter | solution.py:128
Sparse Core Ops, SparseCore 0:
  73.9 16.9 all-gather.9
  93.1 16.6 all-gather.5
  111.9 16.6 all-gather.7
  130.1 45.6 all-gather.11
  247.1 23.7 reduce-scatter.3
  273.8 24.7 reduce-scatter.5
  301.7 24.7 reduce-scatter.7
